TPU v7x, 32 devices: a whole 2x2x4 slice. The times are simulated.
32 devices in a mesh: row: 4 (over y, core), col: 8 (over z, x).
Axes of the slice: x: 2, y: 2, z: 4, core: 2. Of those that a mesh axis runs over, the one named last changes fastest.
Arguments:
- support_views: float32 [256, 4, 3, 1024], P(('row', 'col')), may hold values from -6 to 6
- support_pick: int32 [256], P(('row', 'col')), may hold values from 0 to 3
- target_views: float32 [256, 4, 3, 1024], P(('row', 'col')), may hold values from -6 to 6
- target_pick: int32 [256], P(('row', 'col')), may hold values from 0 to 3
- support_labels: float32 [256, 10], P(('row', 'col')), may hold values from -6 to 6
- target_labels: int32 [256], replicated, may hold values from 0 to 9
Outputs:
- support_grad: float32 [256, 3, 1024], P(('row', 'col'))
- label_grad: float32 [256, 10], P(('row', 'col'))
- loss: float32 [], replicated
All inputs are finite; a program needn't handle non-finite values.
Results may differ from a plain program's by a relative error of at most 0.00055.
Values sent between devices are 32-bit elements; how exact they have to be, the bound alone decides.
No kernel may reach another device: no remote copies, remote signals or barrier semaphores. Data moves between devices by JAX's collectives and lax.ppermute only.
A program may use at most 64 MiB of HBM per device.

v0:
```python
import math
import jax
import jax.numpy as jnp
from jax import lax
from jax.sharding import PartitionSpec as P

SIDE = 32
LAYERS = 3
SUPPORT = 256
bias_variance = 0.1
ridge_scale = 0.1
highest = lax.Precision.HIGHEST


def shifted(surface, offset):
    extent = surface.shape[-1]
    padding = jnp.zeros(surface.shape[:-1] + (abs(offset),), surface.dtype)
    if offset > 0:
        return jnp.concatenate([surface[..., offset:], padding], axis=-1)
    return jnp.concatenate([padding, surface[..., : extent + offset]], axis=-1)


def average(surface):
    column = jnp.arange(surface.shape[-1], dtype=jnp.int32) % SIDE
    rightward = jnp.where(column < SIDE - 1, shifted(surface, 1), 0.0)
    leftward = jnp.where(column > 0, shifted(surface, -1), 0.0)
    across = surface + leftward + rightward
    return (across + shifted(across, SIDE) + shifted(across, -SIDE)) / 9.0


def choose_view(views, picked):
    options = jnp.arange(views.shape[1], dtype=jnp.int32)
    selector = (picked[:, None] == options[None, :]).astype(jnp.float32)
    return jnp.sum(selector[:, :, None, None] * views, axis=1)


def self_maps(images):
    energy = jnp.sum(images * images, axis=1) / images.shape[1]
    current = average(energy) + bias_variance
    stacked = [current]
    for layer in range(1, LAYERS):
        current = average(current) + bias_variance
        stacked.append(current)
    return jnp.stack(stacked, axis=1)


def self_back(images, grad_maps):
    carry = grad_maps[:, -1]
    for layer in range(grad_maps.shape[1] - 2, -1, -1):
        carry = grad_maps[:, layer] + average(carry)
    return average(carry)[:, None, :] * images * (2.0 / images.shape[1])


def arc(kernel_map, first_diag, second_diag):
    scale_map = jnp.sqrt(first_diag * second_diag)
    cosine = jnp.clip(kernel_map / scale_map, -1.0, 1.0)
    sine = jnp.sqrt(1.0 - cosine * cosine)
    angle = jnp.arccos(cosine)
    value = scale_map * (sine + (jnp.pi - angle) * cosine) / jnp.pi
    slope = (jnp.pi - angle) / jnp.pi
    spread = scale_map * sine / (2.0 * jnp.pi)
    return (value, slope, spread)


def pair_forward(first, first_maps, second, second_maps):
    product = first[:, None, 0] * second[None, :, 0]
    for channel in range(1, first.shape[1]):
        product = product + first[:, None, channel] * second[None, :, channel]
    current = average(product / first.shape[1]) + bias_variance
    slopes = []
    spreads = []
    depth = first_maps.shape[1]
    for layer in range(depth):
        value, slope, spread = arc(current, first_maps[:, None, layer], second_maps[None, :, layer])
        slopes.append(slope)
        spreads.append(spread)
        if layer + 1 < depth:
            current = average(value) + bias_variance
    return (jnp.mean(value, axis=-1), slopes, spreads)


def pair_backward(first, first_maps, second, second_maps, weights, want_second):
    kernel, slopes, spreads = pair_forward(first, first_maps, second, second_maps)
    depth = first_maps.shape[1]
    grad = jnp.broadcast_to(weights[:, :, None] / first.shape[-1], slopes[0].shape)
    first_parts = []
    second_parts = []
    for layer in range(depth - 1, -1, -1):
        scaled = grad * spreads[layer]
        first_parts.insert(0, jnp.sum(scaled, axis=1) / first_maps[:, layer])
        if want_second:
            second_parts.insert(0, jnp.sum(scaled, axis=0) / second_maps[:, layer])
        grad = average(grad * slopes[layer])
    first_image = (
        jnp.stack(
            [jnp.sum(grad * second[None, :, channel], axis=1) for channel in range(first.shape[1])],
            axis=1,
        )
        / first.shape[1]
    )
    if not want_second:
        return (first_image, jnp.stack(first_parts, axis=1), None, None)
    second_image = (
        jnp.stack(
            [jnp.sum(grad * first[:, None, channel], axis=0) for channel in range(first.shape[1])],
            axis=1,
        )
        / first.shape[1]
    )
    return (
        first_image,
        jnp.stack(first_parts, axis=1),
        second_image,
        jnp.stack(second_parts, axis=1),
    )


def blocked_kernel(first, first_maps, second, second_maps):
    block_width = math.gcd(second.shape[0], 4)
    block_count = second.shape[0] // block_width

    def one_block(inputs):
        part_images, part_maps = inputs
        kernel, _, _ = pair_forward(first, first_maps, part_images, part_maps)
        return kernel

    pieces = lax.map(
        one_block,
        (
            second.reshape((block_count, block_width) + second.shape[1:]),
            second_maps.reshape((block_count, block_width) + second_maps.shape[1:]),
        ),
    )
    return jnp.transpose(pieces, (1, 0, 2)).reshape(first.shape[0], second.shape[0])


def blocked_backward(first, first_maps, second, second_maps, weights, want_second):
    block_width = math.gcd(second.shape[0], 4)
    block_count = second.shape[0] // block_width
    block_weights = jnp.transpose(
        weights.reshape(first.shape[0], block_count, block_width), (1, 0, 2)
    )

    def one_block(carry, inputs):
        part_images, part_maps, part_weights = inputs
        grad_first, maps_first, grad_second, maps_second = pair_backward(
            first, first_maps, part_images, part_maps, part_weights, want_second
        )
        return ((carry[0] + grad_first, carry[1] + maps_first), (grad_second, maps_second))

    start = (jnp.zeros(first.shape, jnp.float32), jnp.zeros(first_maps.shape, jnp.float32))
    (first_grad, first_map_grad), (second_grad, second_map_grad) = lax.scan(
        one_block,
        start,
        (
            second.reshape((block_count, block_width) + second.shape[1:]),
            second_maps.reshape((block_count, block_width) + second_maps.shape[1:]),
            block_weights,
        ),
    )
    if not want_second:
        return (first_grad, first_map_grad, None, None)
    return (
        first_grad,
        first_map_grad,
        second_grad.reshape(second.shape),
        second_map_grad.reshape(second_maps.shape),
    )


def solve_with(factor, rhs):
    halfway = lax.linalg.triangular_solve(factor, rhs, left_side=True, lower=True)
    return lax.linalg.triangular_solve(
        factor, halfway, left_side=True, lower=True, transpose_a=True
    )


def assemble_folded(tiles, row_count, col_count, own_count, picks):
    span = col_count * own_count
    shaped = tiles.reshape(row_count, col_count, span, picks, own_count)
    block_ids = jnp.arange(row_count, dtype=jnp.int32)
    offsets = jnp.arange(picks, dtype=jnp.int32)
    selector = (
        block_ids[None, None, :] == (block_ids[:, None, None] + offsets[None, :, None]) % row_count
    ).astype(jnp.float32)
    upper = jnp.einsum("rcadk,rdq->raqck", shaped, selector, precision=highest)
    upper = upper.reshape(row_count * span, row_count * span)
    return upper + upper.T - jnp.diag(jnp.diag(upper))


def column_of(matrix, col_index, row_count, col_count, per_device):
    shaped = matrix.reshape(row_count, col_count, per_device, matrix.shape[-1])
    picked = lax.dynamic_index_in_dim(shaped, col_index, 1, keepdims=False)
    return picked.reshape(row_count * per_device, matrix.shape[-1])


def pick_blocks(stacked, row_index, row_count, own_count, picks):
    shaped = stacked.reshape((row_count, own_count) + stacked.shape[1:])
    rolled = jnp.roll(shaped, -row_index, axis=0)[:picks]
    return rolled.reshape((picks * own_count,) + stacked.shape[1:])


def place_blocks(picked, row_index, row_count, own_count, picks):
    shaped = picked.reshape((picks, own_count) + picked.shape[1:])
    padding = jnp.zeros((row_count - picks, own_count) + picked.shape[1:], picked.dtype)
    full = jnp.roll(jnp.concatenate([shaped, padding], axis=0), row_index, axis=0)
    return full.reshape((row_count * own_count,) + picked.shape[1:])


def body(support_views, support_pick, target_views, target_pick, support_labels, target_labels):
    row_count = lax.axis_size("row")
    col_count = lax.axis_size("col")
    row_index = lax.axis_index("row")
    col_index = lax.axis_index("col")
    own_count = support_views.shape[0]
    own_targets = target_views.shape[0]
    channels = support_views.shape[2]
    classes = support_labels.shape[1]
    own_support = choose_view(support_views, support_pick)
    own_target = choose_view(target_views, target_pick)
    support_pack = jnp.concatenate([own_support, self_maps(own_support)], axis=1)
    target_pack = jnp.concatenate([own_target, self_maps(own_target)], axis=1)
    row_pack = lax.all_gather(support_pack, "col", axis=0, tiled=True)
    column_pack, target_block = (
        lax.all_gather(support_pack, "row", axis=0, tiled=True),
        lax.all_gather(target_pack, "row", axis=0, tiled=True),
    )
    row_images = row_pack[:, :channels]
    row_maps = row_pack[:, channels:]
    column_images = column_pack[:, :channels]
    column_maps = column_pack[:, channels:]
    target_images = target_block[:, :channels]
    target_maps = target_block[:, channels:]
    row_start = row_index * col_count * own_count
    row_span = col_count * own_count
    half_count = row_count // 2
    picks = half_count + 1
    chosen_images = pick_blocks(column_images, row_index, row_count, own_count, picks)
    chosen_maps = pick_blocks(column_maps, row_index, row_count, own_count, picks)
    slot_ids = jnp.arange(picks * own_count, dtype=jnp.int32)
    offset_ids = slot_ids // own_count
    inner_ids = slot_ids % own_count
    local_cols = col_index * own_count + inner_ids
    chosen_global = (
        (row_index + offset_ids) % row_count * col_count + col_index
    ) * own_count + inner_ids
    row_ids = jnp.arange(row_span, dtype=jnp.int32)
    keep = jnp.where(
        offset_ids[None, :] == 0,
        row_ids[:, None] <= local_cols[None, :],
        jnp.where(offset_ids[None, :] == half_count, row_index < half_count, True),
    )
    keep_mask = keep.astype(jnp.float32)
    equal_mask = ((offset_ids[None, :] == 0) & (row_ids[:, None] == local_cols[None, :])).astype(
        jnp.float32
    )
    support_tile = blocked_kernel(row_images, row_maps, chosen_images, chosen_maps) * keep_mask
    cross_tile = blocked_kernel(row_images, row_maps, target_images, target_maps)
    onehot_all = (target_labels[:, None] == jnp.arange(classes, dtype=jnp.int32)[None, :]).astype(
        jnp.float32
    ) - 1.0 / classes
    identity = jnp.eye(SUPPORT, dtype=jnp.float32)
    tiles, all_labels = (
        lax.all_gather(support_tile, ("row", "col"), axis=0, tiled=True),
        lax.all_gather(support_labels, ("row", "col"), axis=0, tiled=True),
    )
    support_kernel = assemble_folded(tiles, row_count, col_count, own_count, picks)
    trace_mean = jnp.trace(support_kernel) / SUPPORT
    factor = jnp.linalg.cholesky(support_kernel + ridge_scale * trace_mean * identity)
    alpha = solve_with(factor, all_labels)
    alpha_rows = lax.dynamic_slice_in_dim(alpha, row_start, row_span, 0)
    labels_here = column_of(onehot_all, col_index, row_count, col_count, own_targets)
    predicted = lax.psum(jnp.dot(cross_tile.T, alpha_rows, precision=highest), "row")
    error = predicted - labels_here
    adjoint_part, loss_sum = lax.psum(
        (jnp.dot(cross_tile, error, precision=highest), jnp.sum(error * error)), "col"
    )
    adjoint = lax.all_gather(adjoint_part, "row", axis=0, tiled=True)
    gamma = solve_with(factor, adjoint)
    intersection = jnp.sum(gamma * alpha)
    gamma_rows = lax.dynamic_slice_in_dim(gamma, row_start, row_span, 0)
    cross_weights = jnp.dot(alpha_rows, error.T, precision=highest)
    alpha_chosen = alpha[chosen_global]
    gamma_chosen = gamma[chosen_global]
    folded = -(
        jnp.dot(gamma_rows, alpha_chosen.T, precision=highest)
        + jnp.dot(alpha_rows, gamma_chosen.T, precision=highest)
    )
    support_weights = (
        folded - equal_mask * (0.5 * folded + ridge_scale * intersection / SUPPORT)
    ) * keep_mask
    row_grad, row_map_grad, chosen_grad, chosen_map_grad = blocked_backward(
        row_images, row_maps, chosen_images, chosen_maps, support_weights, True
    )
    col_grad = place_blocks(chosen_grad, row_index, row_count, own_count, picks)
    col_map_grad = place_blocks(chosen_map_grad, row_index, row_count, own_count, picks)
    cross_grad, cross_map_grad, _, _ = blocked_backward(
        row_images, row_maps, target_images, target_maps, cross_weights, False
    )
    row_grad = row_grad + cross_grad
    row_map_grad = row_map_grad + cross_map_grad
    row_send = jnp.concatenate([row_grad, row_map_grad], axis=1)
    col_send = jnp.concatenate([col_grad, col_map_grad], axis=1)
    row_whole = lax.psum(row_send, "col")
    col_whole = lax.psum(col_send, "row")
    row_back = lax.dynamic_slice_in_dim(row_whole, col_index * own_count, own_count, 0)
    col_back = lax.dynamic_slice_in_dim(col_whole, row_index * own_count, own_count, 0)
    combined = row_back + col_back
    support_grad = combined[:, :channels] + self_back(own_support, combined[:, channels:])
    own_start = (row_index * col_count + col_index) * own_count
    label_grad = lax.dynamic_slice_in_dim(gamma, own_start, own_count, 0)
    return (support_grad, label_grad, 0.5 * loss_sum)


def solution(mesh):
    return jax.shard_map(
        body,
        mesh=mesh,
        in_specs=(
            P(("row", "col"), None, None, None),
            P(("row", "col")),
            P(("row", "col"), None, None, None),
            P(("row", "col")),
            P(("row", "col"), None),
            P(),
        ),
        out_specs=(P(("row", "col"), None, None), P(("row", "col"), None), P()),
        check_vma=False,
    )
```

profile of v0, /device:TPU:0, one launch (start us, length us, event | category | flops | bytes accessed | tf_op | source)
XLA Modules:
  0.0 1061.8 jit_solution(16985162748943276678)
XLA Ops:
  13.4 10.3 all_gather.19
  24.6 69.7 %all_gather.22 = f32[256,10]{1,0:T(8,128)S(1)} all-gather(f32[8,10]{1,0:T(8,128)S(1)} %copy-done.22), channel_id=1, replica_groups=mesh['row'=4,'col'=8] {'row','col'}, dimensions={0}, use_global_device_ids=true | all-gather | bytes 10560 | tf_op jit(solution)/shard_map/all_gather | solution.py:265
  94.9 7.8 all_gather.21
  107.6 80.1 %while.70 = (s32[]{:T(128)}, f32[6,64,4]{1,2,0:T(4,128)S(1)}, f32[64,3,1024]{2,0,1:T(8,128)S(1)}, f32[6,4,3,1024]{3,1,2,0:T(4,128)S(1)}, f32[64,3,1024]{2,0,1:T(...) while((s32[]{:T(128)}, f32[6,64,4]{1,2,0:T(4,128)S(1)}, f32[64,3,1024]{2,0,1:T(8,128)S(1)}, ...), condition=%wide.region_4.6_spmd, body=%wide.region_2.5_spmd.sunk | while | flops 19931136 | bytes 54733908 | solution.py:127
  117.9 3.1 multiply_reduce_fusion.27
  131.2 3.1 multiply_reduce_fusion.27
  140.2 3.0 multiply_multiply_fusion.26
  144.4 3.1 multiply_reduce_fusion.27
  157.7 3.1 multiply_reduce_fusion.27
  170.9 3.1 multiply_reduce_fusion.27
  184.2 3.1 multiply_reduce_fusion.27
  187.8 65.5 %all-gather = f32[32,64,24]{1,2,0:T(8,128)S(1)} all-gather(f32[1,64,24]{1,2,0:T(8,128)S(1)} %select_bitcast_fusion.1), channel_id=1, replica_groups=mesh['row'=4,'col'=8] {'row','col'}, dimensions={0}, use_global_device_ids=true | all-gather | bytes 202752 | tf_op jit(solution)/shard_map/all_gather | solution.py:264
  258.8 11.7 %cholesky.49 = f32[128,128]{1,0:T(8,128)S(1)} custom-call(f32[128,128]{1,0:T(8,128)S(1)} %cholesky.115), custom_call_target="Cholesky" | custom-call | tf_op jit(solution)/shard_map/jit(cholesky)/cholesky | solution.py:269
  270.6 9.8 custom-call.17
  280.9 11.7 %cholesky.103 = f32[128,128]{1,0:T(8,128)S(1)} custom-call(f32[128,128]{1,0:T(8,128)S(1)} %convolution_subtract_fusion), custom_call_target="Cholesky" | custom-call | tf_op jit(solution)/shard_map/jit(cholesky)/cholesky | solution.py:269
  295.7 4.3 while.74
  300.6 20.5 %custom-call.29 = f32[2,128,128]{1,2,0:T(8,128)S(1)} custom-call(f32[2,128,128]{2,1,0:T(8,128)} %copy-done.27), custom_call_target="InvertDiagBlocksLowerTriangular" | custom-call | tf_op jit(solution)/shard_map/triangular_solve/custom-call.4 | solution.py:173
  323.0 117.2 %while.71 = (s32[]{:T(128)}, f32[8,64,4]{1,2,0:T(4,128)}, f32[64,3,1024]{2,0,1:T(8,128)S(1)}, f32[8,4,3,1024]{3,1,2,0:T(4,128)}, f32[64,3,1024]{2,0,1:T(8,128)S(1)}, /*index=5*/f32[8,4,3,1024]{3,1,2,0:T(4,128)}, s32[]{:T(128)}) while((s32[]{:T(128)}, f32[8,64,4]{1,2,0:T(4,128)}, f32[64,3,1024]{2,0,1:T(8,128)S(1)}, ...), condition=%wide.region_14.16_spmd, body=%wide.region_12.15_spmd.sunk | while | flops 19931136 | bytes 54733392 | solution.py:127
  334.1 3.1 multiply_reduce_fusion.28
  348.7 3.1 multiply_reduce_fusion.28
  363.4 3.1 multiply_reduce_fusion.28
  378.0 3.1 multiply_reduce_fusion.28
  392.6 3.1 multiply_reduce_fusion.28
  407.2 3.1 multiply_reduce_fusion.28
  421.8 3.1 multiply_reduce_fusion.28
  436.5 3.1 multiply_reduce_fusion.28
  443.1 6.6 psum.35
  454.0 20.6 %all-reduce.111 = (f32[64,10]{0,1:T(8,128)S(1)}, f32[]{:T(128)}) all-reduce(f32[64,10]{0,1:T(8,128)} %fusion.91, f32[]{:T(128)} %multiply_reduce_fusion.19), channel_id=1, replica_groups=mesh['row'=4,'col'=8] {'col'}, use_global_device_ids=true, to_apply=%region_16.20 | all-reduce | flops 641 | bytes 5128 | tf_op jit(solution)/shard_map/psum | solution.py:275
  474.6 5.2 all-gather.1
  489.0 222.6 %while.72 = (s32[]{:T(128)}, f32[64,3,1024]{2,0,1:T(8,128)S(1)}, f32[64,3,1024]{2,0,1:T(8,128)S(1)}, f32[6,4,3,1024]{3,1,0,2:T(4,128)}, f32[6,4,3,1024]{3,1,0,2:...) while((s32[]{:T(128)}, f32[64,3,1024]{2,0,1:T(8,128)S(1)}, ...), condition=%wide.region_31.35_spmd.clone, body=%wide.region_18.34_spmd.clone.sunk | while | flops 38808064 | bytes 129204872 | solution.py:152
  719.3 243.5 %while.73 = (s32[]{:T(128)}, f32[64,3,1024]{2,0,1:T(8,128)S(1)}, f32[64,3,1024]{2,0,1:T(8,128)S(1)}, f32[64,3,1024]{2,0,1:T(8,128)S(1)}, f32[8,4,3,1024]{3,1,2,0...) while((s32[]{:T(128)}, f32[64,3,1024]{2,0,1:T(8,128)S(1)}, ...), condition=%wide.region_39.43_spmd.clone, body=%wide.region_32.42_spmd.clone.sunk | while | flops 36203008 | bytes 120111224 | solution.py:152
  967.8 83.4 %all-reduce.115.cloned.1.call-done = f32[64,6,1024]{2,0,1:T(8,128)} async-done(((f32[64,6,1024]{2,0,1:T(8,128)}), f32[64,6,1024]{2,0,1:T(8,128)}) %all-reduce.115.cloned.1.call-update) | async-done | bytes 1572880 | tf_op jit(solution)/shard_map/psum | solution.py:304
  (1042 shorter events, 632.2 us)
Async XLA Ops:
  7.2 3.4 copy-start.11
  7.2 99.0 %all-gather.4.cloned.1.call-start = ((), (), s32[]{:S(2)}) async-start(), calls=%async_computation | async-start | bytes 1769472 | tf_op jit(solution)/shard_map/all_gather | solution.py:223
  7.2 4.8 copy-start.17
  7.2 4.8 copy-start.19
  10.9 1.6 copy-start.9
  13.4 954.4 %all-reduce.117.cloned.1.call-start = ((), (), s32[]{:S(2)}) async-start(), calls=%async_computation.2 | async-start | bytes 1572864 | tf_op jit(solution)/shard_map/psum | solution.py:305
  23.9 0.7 copy-start.22
  102.8 1.8 copy-start.23
  105.5 82.2 %copy-start.24 = (s32[24]{0:T(128)}, s32[24]{0:T(128)S(1)}, u32[]{:S(2)}) copy-start(s32[24]{0:T(128)S(1)} %fusion.81) | copy-start | bytes 292
  105.5 82.2 %copy-start.25 = (pred[24]{0:T(512)(128)(4,1)}, pred[24]{0:T(512)(128)(4,1)S(1)}, u32[]{:S(2)}) copy-start(pred[24]{0:T(512)(128)(4,1)S(1)} %get-tuple-element.1339) | copy-start | bytes 76
  105.5 82.2 %copy-start.26 = (pred[24]{0:T(512)(128)(4,1)}, pred[24]{0:T(512)(128)(4,1)S(1)}, u32[]{:S(2)}) copy-start(pred[24]{0:T(512)(128)(4,1)S(1)} %get-tuple-element.1340) | copy-start | bytes 76
  187.7 66.6 %copy-start.7 = (f32[6,4,3,1024]{3,1,2,0:T(4,128)}, f32[6,4,3,1024]{3,1,2,0:T(4,128)S(1)}, u32[]{:S(2)}) copy-start(f32[6,4,3,1024]{3,1,2,0:T(4,128)S(1)} %get-tuple-element.2067) | copy-start | bytes 884740
  187.7 66.9 %copy-start.8 = (f32[6,4,3,1024]{3,1,2,0:T(4,128)}, f32[6,4,3,1024]{3,1,2,0:T(4,128)S(1)}, u32[]{:S(2)}) copy-start(f32[6,4,3,1024]{3,1,2,0:T(4,128)S(1)} %get-tuple-element.2068) | copy-start | bytes 884740
  300.0 0.6 copy-start.27
  323.0 126.7 %copy-start.16 = (f32[32,10]{0,1:T(8,128)S(1)}, f32[32,10]{0,1:T(8,128)}, u32[]{:S(2)}) copy-start(f32[32,10]{0,1:T(8,128)} %reshape.516) | copy-start | bytes 3844
  440.2 48.8 %copy-start.2 = (f32[64,3,1024]{2,0,1:T(8,128)S(1)}, f32[64,3,1024]{2,0,1:T(8,128)}, u32[]{:S(2)}) copy-start(f32[64,3,1024]{2,0,1:T(8,128)} %custom-call.22) | copy-start | bytes 2359300
  440.2 48.8 %copy-start.4 = (f32[64,3,1024]{2,0,1:T(8,128)S(1)}, f32[64,3,1024]{2,0,1:T(8,128)}, u32[]{:S(2)}) copy-start(f32[64,3,1024]{2,0,1:T(8,128)} %custom-call.23) | copy-start | bytes 2359300
  441.1 0.6 copy-start.21
  483.9 5.1 copy-start.12
  484.3 4.7 copy-start.14
  711.7 5.8 copy-start.3
  711.7 5.8 copy-start.5
  717.6 1.2 copy-start
  717.6 1.6 copy-start.1
  718.7 332.5 %all-reduce.115.cloned.1.call-start = ((), (), s32[]{:S(2)}) async-start(), calls=%async_computation.1 | async-start | bytes 3145728 | tf_op jit(solution)/shard_map/psum | solution.py:304
  962.8 1.4 copy-start.6
  965.6 0.7 copy-start.13
  965.6 0.7 copy-start.15
  965.6 86.7 %copy-start.18 = (pred[1024]{0:T(1024)(128)(4,1)S(1)}, pred[1024]{0:T(1024)(128)(4,1)}, u32[]{:S(2)}) copy-start(pred[1024]{0:T(1024)(128)(4,1)} %copy-done.17) | copy-start | bytes 3076
  965.6 86.7 %copy-start.20 = (pred[1024]{0:T(1024)(128)(4,1)S(1)}, pred[1024]{0:T(1024)(128)(4,1)}, u32[]{:S(2)}) copy-start(pred[1024]{0:T(1024)(128)(4,1)} %copy-done.19) | copy-start | bytes 3076
  965.6 87.6 %copy-start.10 = (f32[8,3,1024]{2,1,0:T(4,128)S(1)}, f32[8,3,1024]{2,1,0:T(4,128)}, u32[]{:S(2)}) copy-start(f32[8,3,1024]{2,1,0:T(4,128)} %copy-done.9) | copy-start | bytes 294916
Sparse Core Ops, SparseCore 0:
  13.5 47.3 all-gather.3
  718.8 31.1 all-reduce.116
  965.7 85.3 all-reduce.114
where the time goes:
time: 1070 us; the launch traced here: 1060 us
  other arithmetic  564 us (53%)
  blocking collectives  186 us (17%)
  local copies, waits for them, and re-layouts  158 us (15%)
  waiting for transfers between devices  83.5 us (8%)
  loops' own time  41.1 us (4%)
  between operations  19.1 us (2%)
  matrix products  11 us (1%)
    div x56, other arithmetic, arc(): value = scale_map * (sine + (jnp.pi - angle) * cosine) / jnp.pi  165 us
    psum x1, waiting for transfers between devices, body(): row_whole = lax.psum(row_send, 'col')  83.4 us
    add x133, other arithmetic, average(): across = surface + leftward + rightward  83.2 us
    all_gather x1, blocking collectives, body(): lax.all_gather(support_labels, ('row', 'col'), axis=0, tiled=True)  69.7 us
    all_gather x1, blocking collectives, body(): lax.all_gather(support_tile, ('row', 'col'), axis=0, tiled=True)  65.5 us
    mul x40, other arithmetic, pair_backward(): grad = average(grad * slopes[layer])  56.8 us
    reduce_sum x24, other arithmetic, pair_backward(): first_parts.insert(0, jnp.sum(scaled, axis=1) / first_maps[:, layer])  53.7 us
    slice x135, local copies, waits for them, and re-layouts, shifted(): return jnp.concatenate([padding, surface[..., :extent + offset]], axis=-1)  49 us
  transfers between devices with their start and end apart: 3, of which 1 were waited for; matrix products, arithmetic and copies ran while one was open for 24% of the time, Pallas kernels for 0%

commit v1 on v0

--- a/solution.py
+++ b/solution.py
@@ -301,7 +301,11 @@
     row_map_grad = row_map_grad + cross_map_grad
     row_send = jnp.concatenate([row_grad, row_map_grad], axis=1)
     col_send = jnp.concatenate([col_grad, col_map_grad], axis=1)
-    row_whole = lax.psum(row_send, "col")
+    row_whole = row_send
+    for hop in (1, 2, 4):
+        row_whole = row_whole + lax.ppermute(
+            row_whole, "col", [(dev, dev ^ hop) for dev in range(8)]
+        )
     col_whole = lax.psum(col_send, "row")
     row_back = lax.dynamic_slice_in_dim(row_whole, col_index * own_count, own_count, 0)
     col_back = lax.dynamic_slice_in_dim(col_whole, row_index * own_count, own_count, 0)

time: 1070 us -> 1120 us (1.047)
  waiting for transfers between devices: 83.5 us -> 139 us
    ppermute x0 -> x3, waiting for transfers between devices: none -> 106 us  [body(): lax.ppermute(row_whole, 'col', [(dev, dev ^ hop) for dev in range(8)])]
    psum x1 -> x0, waiting for transfers between devices: 83.4 us -> none  [body(): row_whole = lax.psum(row_send, 'col')]
    psum x1, waiting for transfers between devices: 0.02 us -> 33.2 us  [body(): col_whole = lax.psum(col_send, 'row')]
    add x14, other arithmetic: 24.2 us -> 6.91 us  [one_block(): carry[0] + grad_first]
  transfers between devices with their start and end apart: 3 -> 5, of which waited for: 1 -> 4; matrix products, arithmetic and copies ran while one was open for 24% -> 1% of each run, Pallas kernels for 0% -> 0%
where the time goes in v1:
time: 1120 us; the launch traced here: 1110 us
  other arithmetic  568 us (51%)
  blocking collectives  185 us (17%)
  local copies, waits for them, and re-layouts  152 us (14%)
  waiting for transfers between devices  139 us (12%)
  loops' own time  41.7 us (4%)
  between operations  19.5 us (2%)
    div x56, other arithmetic, arc(): value = scale_map * (sine + (jnp.pi - angle) * cosine) / jnp.pi  165 us
    ppermute x3, waiting for transfers between devices, body(): lax.ppermute(row_whole, 'col', [(dev, dev ^ hop) for dev in range(8)])  106 us
    add x133, other arithmetic, average(): across = surface + leftward + rightward  83 us
    all_gather x1, blocking collectives, body(): lax.all_gather(support_labels, ('row', 'col'), axis=0, tiled=True)  69.6 us
    all_gather x1, blocking collectives, body(): lax.all_gather(support_tile, ('row', 'col'), axis=0, tiled=True)  65.5 us
    reduce_sum x24, other arithmetic, pair_backward(): first_parts.insert(0, jnp.sum(scaled, axis=1) / first_maps[:, layer])  64.3 us
    mul x40, other arithmetic, pair_backward(): grad = average(grad * slopes[layer])  60.9 us
    slice x135, local copies, waits for them, and re-layouts, shifted(): return jnp.concatenate([padding, surface[..., :extent + offset]], axis=-1)  49.3 us
  transfers between devices with their start and end apart: 5, of which 4 were waited for; matrix products, arithmetic and copies ran while one was open for 1% of the time, Pallas kernels for 0%

profile of v1, /device:TPU:0, one launch (start us, length us, event | category | flops | bytes accessed | tf_op | source)
XLA Modules:
  0.0 1110.5 jit_solution(9018393693677615733)
XLA Ops:
  13.4 10.3 all_gather.19
  25.0 69.6 %all_gather.22 = f32[256,10]{1,0:T(8,128)S(1)} all-gather(f32[8,10]{1,0:T(8,128)S(1)} %copy-done.32), channel_id=1, replica_groups=mesh['row'=4,'col'=8] {'row','col'}, dimensions={0}, use_global_device_ids=true | all-gather | bytes 10560 | tf_op jit(solution)/shard_map/all_gather | solution.py:265
  95.9 7.8 all_gather.21
  107.4 84.7 %while.70 = (s32[]{:T(128)}, f32[6,64,4]{1,2,0:T(4,128)S(1)}, f32[64,3,1024]{2,0,1:T(8,128)S(1)}, f32[6,4,3,1024]{3,1,2,0:T(4,128)S(1)}, f32[64,3,1024]{2,0,1:T(...) while((s32[]{:T(128)}, f32[6,64,4]{1,2,0:T(4,128)S(1)}, f32[64,3,1024]{2,0,1:T(8,128)S(1)}, ...), condition=%wide.region_4.6_spmd, body=%wide.region_2.5_spmd.sunk | while | flops 19931136 | bytes 54733916 | solution.py:127
  192.2 65.5 %all-gather = f32[32,64,24]{1,2,0:T(8,128)S(1)} all-gather(f32[1,64,24]{1,2,0:T(8,128)S(1)} %select_bitcast_fusion.1), channel_id=1, replica_groups=mesh['row'=4,'col'=8] {'row','col'}, dimensions={0}, use_global_device_ids=true | all-gather | bytes 202752 | tf_op jit(solution)/shard_map/all_gather | solution.py:264
  263.2 11.7 %cholesky.49 = f32[128,128]{1,0:T(8,128)S(1)} custom-call(f32[128,128]{1,0:T(8,128)S(1)} %cholesky.115), custom_call_target="Cholesky" | custom-call | tf_op jit(solution)/shard_map/jit(cholesky)/cholesky | solution.py:269
  275.0 9.8 custom-call.17
  285.4 11.7 %cholesky.103 = f32[128,128]{1,0:T(8,128)S(1)} custom-call(f32[128,128]{1,0:T(8,128)S(1)} %convolution_subtract_fusion), custom_call_target="Cholesky" | custom-call | tf_op jit(solution)/shard_map/jit(cholesky)/cholesky | solution.py:269
  300.1 5.5 while.74
  305.6 20.5 %custom-call.29 = f32[2,128,128]{1,2,0:T(8,128)S(1)} custom-call(f32[2,128,128]{2,1,0:T(8,128)} %get-tuple-element.627), custom_call_target="InvertDiagBlocksLowerTriangular" | custom-call | tf_op jit(solution)/shard_map/triangular_solve/custom-call.4 | solution.py:173
  327.3 106.1 %while.71 = (s32[]{:T(128)}, f32[8,64,4]{1,2,0:T(4,128)S(1)}, f32[64,3,1024]{2,0,1:T(8,128)S(1)}, f32[8,4,3,1024]{3,1,2,0:T(4,128)S(1)}, f32[64,3,1024]{2,0,1:T(...) while((s32[]{:T(128)}, f32[8,64,4]{1,2,0:T(4,128)S(1)}, f32[64,3,1024]{2,0,1:T(8,128)S(1)}, ...), condition=%wide.region_14.16_spmd, body=%wide.region_12.15_spmd.sunk | while | flops 19931136 | bytes 54733916 | solution.py:127
  433.6 5.8 psum.28
  441.0 20.4 %all-reduce.111 = (f32[64,10]{0,1:T(8,128)S(1)}, f32[]{:T(128)}) all-reduce(f32[64,10]{0,1:T(8,128)S(1)} %fusion.92, f32[]{:T(128)} %multiply_reduce_fusion.19), channel_id=1, replica_groups=mesh['row'=4,'col'=8] {'col'}, use_global_device_ids=true, to_apply=%region_16.20 | all-reduce | flops 641 | bytes 5128 | tf_op jit(solution)/shard_map/psum | solution.py:275
  461.4 5.2 all-gather.1
  471.9 236.0 %while.72 = (s32[]{:T(128)}, f32[64,3,1024]{2,0,1:T(8,128)}, f32[64,3,1024]{2,0,1:T(8,128)}, f32[6,4,3,1024]{3,1,0,2:T(4,128)}, f32[6,4,3,1024]{3,1,0,2:T(4,128)...) while((s32[]{:T(128)}, f32[64,3,1024]{2,0,1:T(8,128)}, ...), condition=%wide.region_31.35_spmd.clone, body=%wide.region_18.34_spmd.clone.sunk | while | flops 38808064 | bytes 144933232 | solution.py:152
  707.9 247.1 %while.73 = (s32[]{:T(128)}, f32[64,3,1024]{2,0,1:T(8,128)S(1)}, f32[64,3,1024]{2,0,1:T(8,128)S(1)}, f32[64,3,1024]{2,0,1:T(8,128)S(1)}, f32[8,4,3,1024]{3,1,2,0...) while((s32[]{:T(128)}, f32[64,3,1024]{2,0,1:T(8,128)S(1)}, ...), condition=%wide.region_39.43_spmd.clone, body=%wide.region_32.42_spmd.clone.sunk | while | flops 36203008 | bytes 123257048 | solution.py:152
  726.2 3.5 multiply_reduce_fusion.31
  731.0 3.5 multiply_reduce_fusion.32
  757.1 3.5 multiply_reduce_fusion.31
  761.9 3.5 multiply_reduce_fusion.32
  788.0 3.5 multiply_reduce_fusion.31
  792.7 3.5 multiply_reduce_fusion.32
  818.9 3.5 multiply_reduce_fusion.31
  823.6 3.5 multiply_reduce_fusion.32
  854.5 3.5 multiply_reduce_fusion.32
  885.4 3.5 multiply_reduce_fusion.32
  916.3 3.5 multiply_reduce_fusion.32
  947.2 3.5 multiply_reduce_fusion.32
  956.7 36.6 %collective-permute-done = f32[64,6,1024]{2,0,1:T(8,128)S(1)} collective-permute-done((f32[64,6,1024]{2,0,1:T(8,128)S(1)}, f32[64,6,1024]{2,0,1:T(8,128)S(1)}, u32[]{:S(2)}, u32[]{:S(2)}) %collective-permute-start) | collective-permute-done | bytes 1572896 | tf_op jit(solution)/shard_map/ppermute | solution.py:306
  993.8 35.8 %collective-permute-done.1 = f32[64,6,1024]{2,0,1:T(8,128)S(1)} collective-permute-done((f32[64,6,1024]{2,0,1:T(8,128)S(1)}, f32[64,6,1024]{2,0,1:T(8,128)S(1)}, u32[]{:S(2)}, u32[]{:S(2)}) %collective-permute-start.1) | collective-permute-done | bytes 1572896 | tf_op jit(solution)/shard_map/ppermute | solution.py:306
  1032.8 33.2 %all-reduce.114.cloned.1.call-done = f32[32,6,1024]{2,0,1:T(8,128)} async-done(((f32[32,6,1024]{2,0,1:T(8,128)}), f32[32,6,1024]{2,0,1:T(8,128)}) %all-reduce.114.cloned.1.call-update) | async-done | bytes 786448 | tf_op jit(solution)/shard_map/psum | solution.py:309
  1066.0 33.5 %collective-permute-done.2 = f32[64,6,1024]{2,0,1:T(8,128)} collective-permute-done((f32[64,6,1024]{2,0,1:T(8,128)S(1)}, f32[64,6,1024]{2,0,1:T(8,128)}, u32[]{:S(2)}, u32[]{:S(2)}) %collective-permute-start.2) | collective-permute-done | bytes 1572896 | tf_op jit(solution)/shard_map/ppermute | solution.py:306
  (1171 shorter events, 629.8 us)
Async XLA Ops:
  7.2 3.4 copy-start.20
  7.2 98.8 %all-gather.4.cloned.1.call-start = ((), (), s32[]{:S(2)}) async-start(), calls=%async_computation | async-start | bytes 1769472 | tf_op jit(solution)/shard_map/all_gather | solution.py:223
  7.2 4.8 copy-start.28
  7.2 4.8 copy-start.30
  13.4 1052.7 %all-reduce.114.cloned.1.call-start = ((), (), s32[]{:S(2)}) async-start(), calls=%async_computation.1 | async-start | bytes 1572864 | tf_op jit(solution)/shard_map/psum | solution.py:309
  192.1 66.5 %copy-start.13 = (f32[6,4,3,1024]{3,1,2,0:T(4,128)}, f32[6,4,3,1024]{3,1,2,0:T(4,128)S(1)}, u32[]{:S(2)}) copy-start(f32[6,4,3,1024]{3,1,2,0:T(4,128)S(1)} %get-tuple-element.2065) | copy-start | bytes 884740
  298.7 27.5 %copy-start.19 = (f32[256,10]{1,0:T(8,128)S(1)}, f32[256,10]{1,0:T(8,128)}, u32[]{:S(2)}) copy-start(f32[256,10]{1,0:T(8,128)} %copy-done.18) | copy-start | bytes 30724
  327.3 112.1 %copy-start.27 = (f32[32,10]{0,1:T(8,128)S(1)}, f32[32,10]{0,1:T(8,128)}, u32[]{:S(2)}) copy-start(f32[32,10]{0,1:T(8,128)} %reshape.516) | copy-start | bytes 3844
  433.4 38.4 %copy-start.16 = (f32[8,4,3,1024]{3,1,2,0:T(4,128)}, f32[8,4,3,1024]{3,1,2,0:T(4,128)S(1)}, u32[]{:S(2)}) copy-start(f32[8,4,3,1024]{3,1,2,0:T(4,128)S(1)} %get-tuple-element.2066) | copy-start | bytes 1179652
  433.4 38.4 %copy-start.17 = (f32[8,4,3,1024]{3,1,2,0:T(4,128)}, f32[8,4,3,1024]{3,1,2,0:T(4,128)S(1)}, u32[]{:S(2)}) copy-start(f32[8,4,3,1024]{3,1,2,0:T(4,128)S(1)} %get-tuple-element.2067) | copy-start | bytes 1179652
  467.4 4.5 copy-start.23
  467.8 4.0 copy-start.25
  471.9 236.0 %copy-start = (f32[64,3,1024]{2,0,1:T(8,128)S(1)}, f32[64,3,1024]{2,0,1:T(8,128)}, u32[]{:S(2)}) copy-start(f32[64,3,1024]{2,0,1:T(8,128)} %custom-call.24) | copy-start | bytes 2359300
  471.9 236.0 %copy-start.1 = (f32[64,3,1024]{2,0,1:T(8,128)S(1)}, f32[64,3,1024]{2,0,1:T(8,128)}, u32[]{:S(2)}) copy-start(f32[64,3,1024]{2,0,1:T(8,128)} %custom-call.25) | copy-start | bytes 2359300
  519.5 1.7 copy-start.8
  519.5 1.7 copy-start.9
  552.8 1.7 copy-start.8
  552.8 1.7 copy-start.9
  586.1 1.7 copy-start.8
  586.1 1.7 copy-start.9
  619.4 1.7 copy-start.8
  619.4 1.7 copy-start.9
  652.7 1.7 copy-start.9
  686.0 1.7 copy-start.9
  956.6 36.7 %collective-permute-start = (f32[64,6,1024]{2,0,1:T(8,128)S(1)}, f32[64,6,1024]{2,0,1:T(8,128)S(1)}, u32[]{:S(2)}, u32[]{:S(2)}) collective-permute-start(f32[64,6,1024]{2,0,1:T(8,128)S(1)} %pad_maximum_fusion), channel_id=1, source_target_pairs={{0,1},{1,0},{2,3},{3,2},{4,5},{5,4},{6,7},{7,6},{8,9},{9,8},{10,11... | collective-permute-start | bytes 4718600 | tf_op jit(solution)/shard_map/ppermute | solution.py:306
  993.7 36.2 %copy-start.22 = (f32[6,4,3,1024]{3,1,0,2:T(4,128)S(1)}, f32[6,4,3,1024]{3,1,0,2:T(4,128)}, u32[]{:S(2)}) copy-start(f32[6,4,3,1024]{3,1,0,2:T(4,128)} %get-tuple-element.535) | copy-start | bytes 884740
  993.7 36.4 %copy-start.21 = (f32[6,4,3,1024]{3,1,0,2:T(4,128)S(1)}, f32[6,4,3,1024]{3,1,0,2:T(4,128)}, u32[]{:S(2)}) copy-start(f32[6,4,3,1024]{3,1,0,2:T(4,128)} %get-tuple-element.534) | copy-start | bytes 884740
  993.7 35.8 %collective-permute-start.1 = (f32[64,6,1024]{2,0,1:T(8,128)S(1)}, f32[64,6,1024]{2,0,1:T(8,128)S(1)}, u32[]{:S(2)}, u32[]{:S(2)}) collective-permute-start(f32[64,6,1024]{2,0,1:T(8,128)S(1)} %fusion.94), channel_id=1, source_target_pairs={{0,2},{1,3},{2,0},{3,1},{4,6},{5,7},{6,4},{7,5},{8,10},{9,11},{10,... | collective-permute-start | bytes 4718600 | tf_op jit(solution)/shard_map/ppermute | solution.py:306
  1029.8 69.7 %collective-permute-start.2 = (f32[64,6,1024]{2,0,1:T(8,128)S(1)}, f32[64,6,1024]{2,0,1:T(8,128)}, u32[]{:S(2)}, u32[]{:S(2)}) collective-permute-start(f32[64,6,1024]{2,0,1:T(8,128)S(1)} %add.1688), channel_id=1, source_target_pairs={{0,4},{1,5},{2,6},{3,7},{4,0},{5,1},{6,2},{7,3},{8,12},{9,13},{10,... | collective-permute-start | bytes 4718600 | tf_op jit(solution)/shard_map/ppermute | solution.py:306
  1030.5 70.2 %copy-start.29 = (pred[1024]{0:T(1024)(128)(4,1)S(1)}, pred[1024]{0:T(1024)(128)(4,1)}, u32[]{:S(2)}) copy-start(pred[1024]{0:T(1024)(128)(4,1)} %copy-done.28) | copy-start | bytes 3076
  1030.5 70.2 %copy-start.31 = (pred[1024]{0:T(1024)(128)(4,1)S(1)}, pred[1024]{0:T(1024)(128)(4,1)}, u32[]{:S(2)}) copy-start(pred[1024]{0:T(1024)(128)(4,1)} %copy-done.30) | copy-start | bytes 3076
  1031.5 70.1 %copy-start.15 = (f32[8,3,1024]{2,1,0:T(4,128)S(1)}, f32[8,3,1024]{2,1,0:T(4,128)}, u32[]{:S(2)}) copy-start(f32[8,3,1024]{2,1,0:T(4,128)} %copy-done.14) | copy-start | bytes 294916
  (63 other events, 80.1 us)
Sparse Core Ops, SparseCore 0:
  13.5 47.3 all-gather.3
  1031.6 34.3 all-reduce.113
